TPU v7x, 512 devices: a whole 4x4x16 slice. The times are simulated.
512 devices in a mesh: state: 16 (over x, y_lo, core), snap: 32 (over y_hi, z).
Axes of the slice: x: 4, y: 4 (y_hi: 2, y_lo: 2; y = y_hi * 2 + y_lo), z: 16, core: 2. Of those that a mesh axis runs over, the one named last changes fastest.
Arguments:
- direct: float32 [8192, 4096], P('state', 'snap'), may hold values from -6 to 6
- adjoint: float32 [8192, 4096], P('state', 'snap'), may hold values from -6 to 6
- cell_weight: float32 [8192], P('state'), may hold values from 0.003314563 to 0.03314563
- right_vecs: float32 [4096, 256], P('snap'), may hold values from -0.09375 to 0.09375
- left_vecs: float32 [4096, 256], P('snap'), may hold values from -0.09375 to 0.09375
- inv_root: float32 [256], replicated, may hold values from 0.5 to 2
Outputs:
- gram: float32 [4096, 4096], P('state', 'snap')
- bal_modes: float32 [8192, 256], P(('state', 'snap'))
- adj_modes: float32 [8192, 256], P(('state', 'snap'))
All inputs are finite; a program needn't handle non-finite values.
Results may differ from a plain program's by a relative error of at most 0.00013.
Values sent between devices are 32-bit elements; how exact they have to be, the bound alone decides.
No kernel may reach another device: no remote copies, remote signals or barrier semaphores. Data moves between devices by JAX's collectives and lax.ppermute only.
A program may use at most 64 MiB of HBM per device.

v0:
```python
import jax
import jax.numpy as jnp
from jax import lax
from jax.sharding import PartitionSpec as P


def local(direct, adjoint, cell_weight, right_vecs, left_vecs, inv_root):
    weighted = adjoint * cell_weight[:, None]
    snap_count = lax.axis_size("snap")
    state_count = lax.axis_size("state")
    local_cols = direct.shape[1]
    total_cols = local_cols * snap_count
    product = lax.dot_general(
        lax.all_gather(weighted, "snap", axis=1, tiled=True),
        direct,
        (((0,), (0,)), ((), ())),
        precision=lax.Precision.HIGHEST,
        preferred_element_type=jnp.float32,
    )
    summed = lax.psum(product, "state")
    row_count = total_cols // state_count
    gram = lax.dynamic_slice_in_dim(summed, lax.axis_index("state") * row_count, row_count, 0)
    bal_terms = jnp.dot(
        direct,
        right_vecs * inv_root[None, :],
        precision=lax.Precision.HIGHEST,
        preferred_element_type=jnp.float32,
    )
    adj_terms = jnp.dot(
        adjoint,
        left_vecs * inv_root[None, :],
        precision=lax.Precision.HIGHEST,
        preferred_element_type=jnp.float32,
    )
    bal_whole, adj_whole = lax.psum((bal_terms, adj_terms), "snap")
    mode_rows = direct.shape[0] // snap_count
    first_row = lax.axis_index("snap") * mode_rows
    bal_modes = lax.dynamic_slice_in_dim(bal_whole, first_row, mode_rows, 0)
    adj_modes = lax.dynamic_slice_in_dim(adj_whole, first_row, mode_rows, 0)
    return (gram, bal_modes, adj_modes)


def solution(mesh):
    in_specs = (
        P("state", "snap"),
        P("state", "snap"),
        P("state"),
        P("snap", None),
        P("snap", None),
        P(),
    )
    out_specs = (P("state", "snap"), P(("state", "snap"), None), P(("state", "snap"), None))
    return jax.shard_map(local, mesh=mesh, in_specs=in_specs, out_specs=out_specs, check_vma=False)
```

profile of v0, /device:TPU:1, one launch (start us, length us, event | category | flops | bytes accessed | tf_op | source)
XLA Modules:
  0.0 670.3 jit_solution(1685941438438533524)
XLA Ops:
  7.2 0.0 copy-start
  7.2 0.0 all-gather.2.cloned.1.call-start
  7.2 1.8 broadcast_multiply_fusion
  9.1 0.0 all-gather.2.cloned.1.call-update
  9.1 0.0 all-reduce.6.cloned.1.call-start
  9.1 2.5 convolution_bitcast_fusion
  11.6 0.0 copy-done
  11.6 2.3 convolution_bitcast_fusion.1
  13.9 0.0 all-reduce.6.cloned.1.call-update
  14.0 0.0 all-reduce.4.cloned.1.call-start
  14.0 201.6 %all-gather.2.cloned.1.call-done = f32[512,4096]{1,0:T(8,128)} async-done(((f32[512,128]{1,0:T(8,128)}), f32[512,4096]{1,0:T(8,128)}) %all-gather.2.cloned.1.call-update) | async-done | bytes 8388624 | tf_op jit(solution)/shard_map/all_gather | solution.py:14
  215.6 16.5 %fusion.4 = f32[4096,128]{1,0:T(8,128)} fusion(f32[512,4096]{1,0:T(8,128)} %all-gather.2.cloned.1.call-done, f32[512,128]{1,0:T(8,128)S(1)} %copy-done), kind=kOutput, calls=%fused_computation.10 | convolution fusion | flops 3221225472 | bytes 10747904 | tf_op jit(solution)/shard_map/dot_general | solution.py:13
  232.1 0.0 all-reduce.4.cloned.1.call-update
  232.2 272.2 %all-reduce.6.cloned.1.call-done = (f32[512,256]{0,1:T(8,128)}, f32[512,256]{0,1:T(8,128)}) async-done(((f32[512,256]{0,1:T(8,128)}, f32[512,256]{0,1:T(8,128)}), (f32[512,256]{0,1:T(8,128)}, f32[512,256]{0,1:T(8,128)})) %all-reduce.6.cloned.1.call-update) | async-done | bytes 1048592 | tf_op jit(solution)/shard_map/psum | solution.py:35
  504.4 1.1 constant_dynamic-slice_fusion
  505.5 0.7 copy.9
  506.2 0.7 copy.10
  506.9 155.3 %all-reduce.4.cloned.1.call-done = f32[4096,128]{1,0:T(8,128)} async-done(((f32[4096,128]{1,0:T(8,128)}), f32[4096,128]{1,0:T(8,128)}) %all-reduce.4.cloned.1.call-update) | async-done | bytes 2097168 | tf_op jit(solution)/shard_map/psum | solution.py:20
  662.2 1.6 constant_dynamic-slice_fusion.2
Async XLA Ops:
  7.2 4.4 copy-start
  7.2 208.4 %all-gather.2.cloned.1.call-start = ((), (), s32[]{:S(2)}) async-start(), calls=%async_computation | async-start | bytes 8650752 | tf_op jit(solution)/shard_map/all_gather | solution.py:14
  9.1 495.3 %all-reduce.6.cloned.1.call-start = ((), (), s32[]{:S(2)}) async-start(), calls=%async_computation.2 | async-start | bytes 2097152 | tf_op jit(solution)/shard_map/psum | solution.py:35
  14.0 648.2 %all-reduce.4.cloned.1.call-start = ((), (), s32[]{:S(2)}) async-start(), calls=%async_computation.1 | async-start | bytes 4194304 | tf_op jit(solution)/shard_map/psum | solution.py:20
Sparse Core Ops, SparseCore 0:
  10.9 204.6 all-gather.1
  218.5 285.8 all-reduce.5
  507.3 154.8 all-reduce.3
where the time goes:
time: 670 us
  waiting for transfers between devices  629 us (94%)
  matrix products  21.3 us (3%)
  between operations  13.8 us (2%)
    psum x1, waiting for transfers between devices, local(): bal_whole, adj_whole = lax.psum((bal_terms, adj_terms), 'snap')  272 us
    all_gather x1, waiting for transfers between devices, local(): lax.all_gather(weighted, 'snap', axis=1, tiled=True)  202 us
    psum x1, waiting for transfers between devices, local(): summed = lax.psum(product, 'state')  155 us
    dot_general x1, matrix products, local(): lax.dot_general(lax.all_gather(weighted, 'snap', axis=1, tiled=True), dir...  16.5 us
  transfers between devices with their start and end apart: 3, of which 3 were waited for; matrix products, arithmetic and copies ran while one was open for 4% of the time, Pallas kernels for 0%

commit v1 on v0

--- a/solution.py
+++ b/solution.py
@@ -17,7 +17,8 @@
         precision=lax.Precision.HIGHEST,
         preferred_element_type=jnp.float32,
     )
-    summed = lax.psum(product, "state")
+    pieces = lax.all_gather(product, "state", axis=0, tiled=False)
+    summed = pieces.sum(axis=0)
     row_count = total_cols // state_count
     gram = lax.dynamic_slice_in_dim(summed, lax.axis_index("state") * row_count, row_count, 0)
     bal_terms = jnp.dot(

time: 670 us -> 720 us (1.075)
  waiting for transfers between devices: 629 us -> 668 us
  other arithmetic: 1.85 us -> 13.6 us
    all_gather x0 -> x1, waiting for transfers between devices: none -> 194 us  [local(): pieces = lax.all_gather(product, 'state', axis=0, tiled=False)]
    psum x1 -> x0, waiting for transfers between devices: 155 us -> none  [local(): summed = lax.psum(product, 'state')]
    reduce_sum x0 -> x1, other arithmetic: none -> 11.7 us  [local(): summed = pieces.sum(axis=0)]
  transfers between devices with their start and end apart: 3 -> 3, of which waited for: 3 -> 3; matrix products, arithmetic and copies ran while one was open for 4% -> 3% of each run, Pallas kernels for 0% -> 0%
where the time goes in v1:
time: 720 us
  waiting for transfers between devices  668 us (93%)
  matrix products  21.4 us (3%)
  between operations  13.8 us (2%)
  other arithmetic  13.6 us (2%)
    psum x1, waiting for transfers between devices, local(): bal_whole, adj_whole = lax.psum((bal_terms, adj_terms), 'snap')  272 us
    all_gather x1, waiting for transfers between devices, local(): lax.all_gather(weighted, 'snap', axis=1, tiled=True)  202 us
    all_gather x1, waiting for transfers between devices, local(): pieces = lax.all_gather(product, 'state', axis=0, tiled=False)  194 us
    dot_general x1, matrix products, local(): lax.dot_general(lax.all_gather(weighted, 'snap', axis=1, tiled=True), dir...  16.6 us
  transfers between devices with their start and end apart: 3, of which 3 were waited for; matrix products, arithmetic and copies ran while one was open for 3% of the time, Pallas kernels for 0%

profile of v1, /device:TPU:1, one launch (start us, length us, event | category | flops | bytes accessed | tf_op | source)
XLA Modules:
  0.0 719.8 jit_solution(18445614418700292004)
XLA Ops:
  7.2 0.0 copy-start
  7.2 0.0 all-gather.4.cloned.1.call-start
  7.2 1.8 broadcast_multiply_fusion
  9.1 0.0 all-gather.4.cloned.1.call-update
  9.1 0.0 all-reduce.3.cloned.1.call-start
  9.1 2.5 convolution_bitcast_fusion
  11.6 0.0 copy-done
  11.6 2.3 convolution_bitcast_fusion.1
  14.0 0.0 all-reduce.3.cloned.1.call-update
  14.0 0.0 all-gather.6.cloned.1.call-start
  14.0 201.6 %all-gather.4.cloned.1.call-done = f32[512,4096]{1,0:T(8,128)} async-done(((f32[512,128]{1,0:T(8,128)}), f32[512,4096]{1,0:T(8,128)}) %all-gather.4.cloned.1.call-update) | async-done | bytes 8388624 | tf_op jit(solution)/shard_map/all_gather | solution.py:14
  215.6 16.6 %fusion.4 = f32[4096,128]{1,0:T(8,128)} fusion(f32[512,4096]{1,0:T(8,128)} %all-gather.4.cloned.1.call-done, f32[512,128]{1,0:T(8,128)S(1)} %copy-done), kind=kOutput, calls=%fused_computation.10 | convolution fusion | flops 3221225472 | bytes 10747904 | tf_op jit(solution)/shard_map/dot_general | solution.py:13
  232.2 0.0 all-gather.6.cloned.1.call-update
  232.2 272.2 %all-reduce.3.cloned.1.call-done = (f32[512,256]{0,1:T(8,128)}, f32[512,256]{0,1:T(8,128)}) async-done(((f32[512,256]{0,1:T(8,128)}, f32[512,256]{0,1:T(8,128)}), (f32[512,256]{0,1:T(8,128)}, f32[512,256]{0,1:T(8,128)})) %all-reduce.3.cloned.1.call-update) | async-done | bytes 1048592 | tf_op jit(solution)/shard_map/psum | solution.py:36
  504.4 1.1 constant_dynamic-slice_fusion
  505.5 0.7 copy.9
  506.2 0.7 copy.10
  506.9 194.0 %all-gather.6.cloned.1.call-done = f32[65536,128]{1,0:T(8,128)} async-done(((f32[4096,128]{1,0:T(8,128)}), f32[65536,128]{1,0:T(8,128)}) %all-gather.6.cloned.1.call-update) | async-done | bytes 33554448 | tf_op jit(solution)/shard_map/all_gather | solution.py:20
  700.8 11.7 %reduce_sum.9 = f32[4096,128]{1,0:T(8,128)S(1)} reduce(f32[16,4096,128]{2,1,0:T(8,128)} %bitcast.9, f32[]{:T(128)} %constant.3.clone.1), dimensions={0}, to_apply=%region_0.0 | reduce | flops 7864320 | bytes 35651588 | tf_op jit(solution)/shard_map/reduce_sum | solution.py:21
  712.6 0.7 constant_dynamic-slice_fusion.2
Async XLA Ops:
  7.2 4.5 copy-start
  7.2 208.4 %all-gather.4.cloned.1.call-start = ((), (), s32[]{:S(2)}) async-start(), calls=%async_computation | async-start | bytes 8650752 | tf_op jit(solution)/shard_map/all_gather | solution.py:14
  9.1 495.3 %all-reduce.3.cloned.1.call-start = ((), (), s32[]{:S(2)}) async-start(), calls=%async_computation.2 | async-start | bytes 2097152 | tf_op jit(solution)/shard_map/psum | solution.py:36
  14.0 686.8 %all-gather.6.cloned.1.call-start = ((), (), s32[]{:S(2)}) async-start(), calls=%async_computation.1 | async-start | bytes 35651584 | tf_op jit(solution)/shard_map/all_gather | solution.py:20
Sparse Core Ops, SparseCore 0:
  10.9 204.6 all-gather.3
  218.5 285.8 all-reduce.2
  506.5 194.2 all-gather.5
